TPU v7x, 32 devices: a whole 2x2x4 slice. The times are simulated.
32 devices in a mesh: row: 4 (over z), col: 8 (over y, x, core).
Axes of the slice: x: 2, y: 2, z: 4, core: 2. Of those that a mesh axis runs over, the one named last changes fastest.
Arguments:
- occupations: int32 [4096, 128], P('row'), may hold values from 0 to 2
- table: float32 [384, 1024], replicated, may hold values from -0.5 to 0.5
- weights: float32 [2, 1024, 4096], P(None, None, 'col'), may hold values from -0.1875 to 0.1875
- biases: float32 [2, 4096], P(None, 'col'), may hold values from -6 to 6
- heads: float32 [2, 4096], P(None, 'col'), may hold values from -18 to 18
- energies: float32 [4096], P('row'), may hold values from -6 to 6
Outputs:
- schur: float32 [4096, 4096], P('row', 'col')
- solved_rhs: float32 [4096], P('row')
All inputs are finite; a program needn't handle non-finite values.
Results may differ from a plain program's by a relative error of at most 0.0034.
Values may be sent and summed in bfloat16 or wider, within the bound.
A program may use at most 128 MiB of HBM per device.

v0:
```python
import math

import jax
import jax.numpy as jnp
from jax import lax
from jax.sharding import PartitionSpec as P

norm_eps = 1e-06
diag_shift = 0.05


def broadcast(block, axis, holder):
    block = jnp.where(lax.axis_index(axis) == holder, block, jnp.zeros_like(block))
    return lax.psum(block, axis)


def jacobian(occupations, table, weights, biases, heads):
    onehot = jnp.concatenate(
        [
            (occupations == 0).astype(jnp.float32),
            (occupations == 1).astype(jnp.float32),
            (occupations == 2).astype(jnp.float32),
        ],
        axis=1,
    )
    embedded = jnp.dot(
        onehot, table, precision=lax.Precision.HIGHEST, preferred_element_type=jnp.float32
    )
    embedded = embedded * lax.rsqrt(
        jnp.mean(embedded * embedded, axis=-1, keepdims=True) + norm_eps
    )
    blocks = []
    for panel_index in range(2):
        hidden = (
            jnp.dot(
                embedded,
                weights[panel_index],
                precision=lax.Precision.HIGHEST,
                preferred_element_type=jnp.float32,
            )
            + biases[panel_index]
        )
        blocks.append(heads[panel_index] * jax.nn.sigmoid(hidden))
    return jnp.concatenate(blocks, axis=1)


def on_device(occupations, table, weights, biases, heads, energies):
    row_count = occupations.shape[0]
    row_devices = lax.axis_size("row")
    col_devices = lax.axis_size("col")
    sample_total = row_count * row_devices
    panel_width = sample_total // col_devices
    derivs = jacobian(occupations, table, weights, biases, heads)
    col_sums = lax.psum(jnp.sum(derivs, axis=0), "row")
    centered = ((derivs - col_sums / sample_total) * (1.0 / math.sqrt(sample_total))).astype(
        jnp.bfloat16
    )
    own_rows = lax.all_gather(centered, "col", axis=1, tiled=True)
    every_sample = lax.all_gather(centered, "row", axis=0, tiled=True)
    partner = lax.all_to_all(every_sample, "col", split_axis=0, concat_axis=1, tiled=True)
    kernel = lax.dot_general(
        own_rows, partner, (((1,), (1,)), ((), ())), preferred_element_type=jnp.float32
    )
    row_ids = lax.axis_index("row") * row_count + lax.iota(jnp.int32, row_count)
    col_ids = lax.axis_index("col") * panel_width + lax.iota(jnp.int32, panel_width)
    kernel = kernel + jnp.where(row_ids[:, None] == col_ids[None, :], diag_shift, 0.0).astype(
        jnp.float32
    )
    right_side = energies
    for panel_index in range(2):
        start_global = panel_index * panel_width
        root_row = start_global // row_count
        offset = start_global % row_count
        top_block, top_side = (
            broadcast(kernel[offset : offset + panel_width], "row", root_row),
            broadcast(right_side[offset : offset + panel_width], "row", root_row),
        )
        column, diag_block = (
            broadcast(kernel, "col", panel_index),
            broadcast(top_block, "col", panel_index),
        )
        factor = jnp.linalg.cholesky(diag_block)
        left_rows = lax.linalg.triangular_solve(
            factor, column, left_side=False, lower=True, transpose_a=True
        )
        right_rows = lax.linalg.triangular_solve(
            factor, top_block.T, left_side=False, lower=True, transpose_a=True
        )
        kernel = kernel - lax.dot_general(
            left_rows,
            right_rows,
            (((1,), (1,)), ((), ())),
            precision=lax.Precision.HIGHEST,
            preferred_element_type=jnp.float32,
        )
        solved = lax.linalg.triangular_solve(factor, top_side[:, None], left_side=True, lower=True)[
            :, 0
        ]
        right_side = right_side - jnp.dot(
            left_rows, solved, precision=lax.Precision.HIGHEST, preferred_element_type=jnp.float32
        )
        placed = right_side.at[offset : offset + panel_width].set(solved)
        right_side = jnp.where(lax.axis_index("row") == root_row, placed, right_side)
    return (kernel, right_side)


def solution(mesh):
    placed = (P("row", None), P(), P(None, None, "col"), P(None, "col"), P(None, "col"), P("row"))
    return jax.shard_map(
        on_device,
        mesh=mesh,
        in_specs=placed,
        out_specs=(P("row", "col"), P("row")),
        check_vma=False,
    )
```

profile of v0, /device:TPU:0, one launch (start us, length us, event | category | flops | bytes accessed | tf_op | source)
XLA Modules:
  0.0 969.1 jit_solution(3831402307478594253)
XLA Ops:
  13.9 12.5 %divide_multiply_fusion.1 = f32[1024,512]{0,1:T(8,128)S(1)} fusion(f32[2,1024,512]{2,1,0:T(8,128)} %param.19, f32[1024,1024]{0,1:T(8,128)} %get-tuple-element.136, f32[1024]{0:T(1024)S(1)} %add_rsqrt_fusion, f32[512]{0:T(512)S(1)} %bitcast.291, f32[512]{0:T(512)S(1)} %bitcast.290), kind=kOutput, calls=%fused_computation.20 | convolution fusion | flops 6446120960 | bytes 8396800 | tf_op jit(solution)/shard_map/dot_general | solution.py:35
  35.6 13.7 %all-reduce.3 = (f32[1024]{0:T(1024)S(1)}, f32[512,1]{0,1:T(1,128)S(1)}) all-reduce(f32[1024]{0:T(1024)S(1)} %fusion.4, f32[512,1]{0,1:T(1,128)S(1)} %bitcast.282), channel_id=1, replica_groups=mesh['row'=4,'col'=8] {'row'}, use_global_device_ids=true, to_apply=%region_2.0 | all-reduce | flops 1536 | bytes 12288 | tf_op jit(solution)/shard_map/psum | solution.py:54
  54.1 147.2 %all-gather.5.cloned.1.call-done = bf16[4096,1024]{0,1:T(8,128)(2,1)} async-done(((bf16[1024,1024]{0,1:T(8,128)(2,1)}), bf16[4096,1024]{0,1:T(8,128)(2,1)}) %all-gather.5.cloned.1.call-update) | async-done | bytes 8388624 | tf_op jit(solution)/shard_map/all_gather | solution.py:59
  214.2 126.8 %all-to-all-done = bf16[8,512,1024]{1,2,0:T(8,128)(2,1)} async-done(((bf16[8,512,1024]{1,2,0:T(8,128)(2,1)}), bf16[8,512,1024]{1,2,0:T(8,128)(2,1)}, u32[]{:S(2)}, u32[]{:S(2)}) %all-to-all-start) | async-done | bytes 8388640 | tf_op jit(solution)/shard_map/all_to_all | solution.py:60
  341.0 32.8 %all-gather.3.cloned.1.call-done = bf16[1024,8192]{0,1:T(8,128)(2,1)} async-done(((bf16[1024,1024]{0,1:T(8,128)(2,1)}), bf16[1024,8192]{0,1:T(8,128)(2,1)}) %all-gather.3.cloned.1.call-update) | async-done | bytes 16777232 | tf_op jit(solution)/shard_map/all_gather | solution.py:58
  373.8 15.9 %broadcast_select_fusion.1 = (f32[1024,512]{0,1:T(8,128)}, f32[1024,512]{0,1:T(8,128)S(1)}) fusion(pred[]{:T(512)S(6)} %eq.56, s32[512]{0:T(512)S(1)} %iota_add_fusion.1, s32[1024]{0:T(1024)S(1)} %iota_add_fusion, bf16[1024,8192]{0,1:T(8,128)(2,1)} %all-gather.3.cloned.1.call-done, bf16[512,8192]{0,1:T(8,128)(2,1)} %bitcast.7), kind=kOutput, calls=%fused_computation.118 | convolution fusion | flops 8592031744 | bytes 29366272 | tf_op jit(solution)/shard_map/dot_general | solution.py:61
  392.2 51.6 %all-reduce.9.cloned.1.call-done = f32[512,512]{0,1:T(8,128)} async-done(((f32[512,512]{0,1:T(8,128)}), f32[512,512]{0,1:T(8,128)}) %all-reduce.9.cloned.1.call-update) | async-done | bytes 1048592 | tf_op jit(solution)/shard_map/psum | solution.py:14
  446.6 69.6 %all-reduce.15.cloned.1.call-done = (f32[1024,512]{0,1:T(8,128)}, f32[512,512]{0,1:T(8,128)}) async-done(((f32[1024,512]{0,1:T(8,128)}, f32[512,512]{0,1:T(8,128)}), (f32[1024,512]{0,1:T(8,128)}, f32[512,512]{0,1:T(8,128)})) %all-reduce.15.cloned.1.call-update) | async-done | bytes 3145744 | tf_op jit(solution)/shard_map/psum | solution.py:14
  519.1 11.7 %cholesky.286 = f32[128,128]{1,0:T(8,128)S(1)} custom-call(f32[128,128]{1,0:T(8,128)S(1)} %cholesky.426), custom_call_target="Cholesky" | custom-call | tf_op jit(solution)/shard_map/jit(cholesky)/cholesky | solution.py:82
  543.3 11.7 %cholesky.305 = f32[128,128]{1,0:T(8,128)S(1)} custom-call(f32[128,128]{1,0:T(8,128)S(1)} %cholesky.430), custom_call_target="Cholesky" | custom-call | tf_op jit(solution)/shard_map/jit(cholesky)/cholesky | solution.py:82
  555.1 10.0 %custom-call.36 = f32[1,128,128]{1,2,0:T(8,128)S(1)} custom-call(f32[1,128,128]{2,1,0:T(8,128)S(1)} %get-tuple-element.127), custom_call_target="InvertDiagBlocksLowerTriangular" | custom-call | tf_op jit(solution)/shard_map/jit(cholesky)/cholesky | solution.py:82
  566.6 11.7 %cholesky.326 = f32[128,128]{1,0:T(8,128)S(1)} custom-call(f32[128,128]{1,0:T(8,128)S(1)} %cholesky.435), custom_call_target="Cholesky" | custom-call | tf_op jit(solution)/shard_map/jit(cholesky)/cholesky | solution.py:82
  590.3 11.7 %cholesky.343 = f32[128,128]{1,0:T(8,128)S(1)} custom-call(f32[128,128]{1,0:T(8,128)S(1)} %convolution_subtract_fusion.17), custom_call_target="Cholesky" | custom-call | tf_op jit(solution)/shard_map/jit(cholesky)/cholesky | solution.py:82
  614.7 39.3 %custom-call.38 = f32[4,128,128]{1,2,0:T(8,128)S(1)} custom-call(f32[4,128,128]{2,1,0:T(8,128)S(1)} %get-tuple-element.72), custom_call_target="InvertDiagBlocksLowerTriangular" | custom-call | tf_op jit(solution)/shard_map/triangular_solve/custom-call.3 | solution.py:83
  676.3 51.5 %all-reduce.11.cloned.1.call-done = f32[512,512]{0,1:T(8,128)} async-done(((f32[512,512]{0,1:T(8,128)}), f32[512,512]{0,1:T(8,128)}) %all-reduce.11.cloned.1.call-update) | async-done | bytes 1048592 | tf_op jit(solution)/shard_map/psum | solution.py:14
  731.1 10.1 %psum.71 = f32[512,1]{0,1:T(1,128)S(1)} all-reduce(f32[512,1]{0,1:T(1,128)S(1)} %bitcast.285), channel_id=1, replica_groups=mesh['row'=4,'col'=8] {'row'}, use_global_device_ids=true, to_apply=%region_18.23 | all-reduce | flops 512 | bytes 4096 | tf_op jit(solution)/shard_map/psum | solution.py:14
  741.3 58.9 %all-reduce.13.cloned.1.call-done = (f32[1024,512]{0,1:T(8,128)}, f32[512,512]{0,1:T(8,128)}) async-done(((f32[1024,512]{0,1:T(8,128)}, f32[512,512]{0,1:T(8,128)}), (f32[1024,512]{0,1:T(8,128)}, f32[512,512]{0,1:T(8,128)})) %all-reduce.13.cloned.1.call-update) | async-done | bytes 3145744 | tf_op jit(solution)/shard_map/psum | solution.py:14
  803.1 11.7 %cholesky.358 = f32[128,128]{1,0:T(8,128)S(1)} custom-call(f32[128,128]{1,0:T(8,128)S(1)} %cholesky.439), custom_call_target="Cholesky" | custom-call | tf_op jit(solution)/shard_map/jit(cholesky)/cholesky | solution.py:82
  815.0 9.8 %custom-call.40 = f32[1,128,128]{1,2,0:T(8,128)S(1)} custom-call(f32[1,128,128]{2,1,0:T(8,128)S(1)} %get-tuple-element.120), custom_call_target="InvertDiagBlocksLowerTriangular" | custom-call | tf_op jit(solution)/shard_map/jit(cholesky)/cholesky | solution.py:82
  827.3 11.7 %cholesky.377 = f32[128,128]{1,0:T(8,128)S(1)} custom-call(f32[128,128]{1,0:T(8,128)S(1)} %cholesky.443), custom_call_target="Cholesky" | custom-call | tf_op jit(solution)/shard_map/jit(cholesky)/cholesky | solution.py:82
  840.4 10.2 %custom-call.41 = f32[1,128,128]{1,2,0:T(8,128)S(1)} custom-call(f32[1,128,128]{2,1,0:T(8,128)S(1)} %get-tuple-element.117), custom_call_target="InvertDiagBlocksLowerTriangular" | custom-call | tf_op jit(solution)/shard_map/jit(cholesky)/cholesky | solution.py:82
  852.2 11.7 %cholesky.398 = f32[128,128]{1,0:T(8,128)S(1)} custom-call(f32[128,128]{1,0:T(8,128)S(1)} %cholesky.448), custom_call_target="Cholesky" | custom-call | tf_op jit(solution)/shard_map/jit(cholesky)/cholesky | solution.py:82
  875.9 11.7 %cholesky.415 = f32[128,128]{1,0:T(8,128)S(1)} custom-call(f32[128,128]{1,0:T(8,128)S(1)} %convolution_subtract_fusion.16), custom_call_target="Cholesky" | custom-call | tf_op jit(solution)/shard_map/jit(cholesky)/cholesky | solution.py:82
  899.3 39.3 %custom-call.43 = f32[4,128,128]{1,2,0:T(8,128)S(1)} custom-call(f32[4,128,128]{2,1,0:T(8,128)S(1)} %get-tuple-element.74), custom_call_target="InvertDiagBlocksLowerTriangular" | custom-call | tf_op jit(solution)/shard_map/triangular_solve/custom-call.3 | solution.py:83
  (204 shorter events, 171.6 us)
Async XLA Ops:
  7.2 1.6 copy-start
  7.2 194.1 %all-gather.5.cloned.1.call-start = ((), (), s32[]{:S(2)}) async-start(), calls=%async_computation.2 | async-start | bytes 10485760 | tf_op jit(solution)/shard_map/all_gather | solution.py:59
  8.7 5.1 copy-start.19
  8.7 5.1 copy-start.20
  13.8 12.6 %copy-start.21 = (f32[2,1024,512]{2,1,0:T(8,128)S(1)}, f32[2,1024,512]{2,1,0:T(8,128)}, u32[]{:S(2)}) copy-start(f32[2,1024,512]{2,1,0:T(8,128)} %param.19) | copy-start | bytes 12582916
  13.9 12.6 %copy-start.22 = (f32[1024,1024]{0,1:T(8,128)S(1)}, f32[1024,1024]{0,1:T(8,128)}, u32[]{:S(2)}) copy-start(f32[1024,1024]{0,1:T(8,128)} %get-tuple-element.136) | copy-start | bytes 12582916
  26.4 7.2 copy-start.4
  53.3 320.5 %all-gather.3.cloned.1.call-start = ((), (), s32[]{:S(2)}) async-start(), calls=%async_computation.1 | async-start | bytes 18874368 | tf_op jit(solution)/shard_map/all_gather | solution.py:58
  209.1 131.9 %all-to-all-start = ((bf16[8,512,1024]{1,2,0:T(8,128)(2,1)}), bf16[8,512,1024]{1,2,0:T(8,128)(2,1)}, u32[]{:S(2)}, u32[]{:S(2)}) async-start(bf16[8,512,1024]{1,2,0:T(8,128)(2,1)} %bitcast.258), calls=%async_computation | async-start | bytes 16777216 | tf_op jit(solution)/shard_map/all_to_all | solution.py:60
  214.1 229.6 %all-reduce.9.cloned.1.call-start = ((), (), s32[]{:S(2)}) async-start(), calls=%async_computation.3 | async-start | bytes 2097152 | tf_op jit(solution)/shard_map/psum | solution.py:14
  389.7 1.4 copy-start.6
  392.2 124.1 %all-reduce.15.cloned.1.call-start = ((), (), s32[]{:S(2)}) async-start(), calls=%async_computation.6 | async-start | bytes 6291456 | tf_op jit(solution)/shard_map/psum | solution.py:14
  446.1 281.7 %all-reduce.11.cloned.1.call-start = ((), (), s32[]{:S(2)}) async-start(), calls=%async_computation.4 | async-start | bytes 2097152 | tf_op jit(solution)/shard_map/psum | solution.py:14
  516.2 1.7 copy-start.9
  660.3 2.9 copy-start.11
  663.3 4.8 copy-start.14
  664.3 3.7 copy-start.7
  673.2 1.4 copy-start.2
  675.7 124.5 %all-reduce.13.cloned.1.call-start = ((), (), s32[]{:S(2)}) async-start(), calls=%async_computation.5 | async-start | bytes 6291456 | tf_op jit(solution)/shard_map/psum | solution.py:14
  800.2 1.7 copy-start.8
  939.4 4.7 copy-start.16
  946.6 1.8 copy-start.10
  949.5 3.8 copy-start.3
  953.3 8.7 copy-start.1
  (6 other events, 5.6 us)
Sparse Core Ops, SparseCore 0:
  53.5 147.7 all-gather.4
  203.1 170.6 all-gather.2
  392.3 51.4 all-reduce.8
  447.6 68.6 all-reduce.14
  675.8 51.9 all-reduce.10
  731.6 68.6 all-reduce.12
where the time goes:
time: 975 us; the launch traced here: 969 us
  waiting for transfers between devices  539 us (55%)
  other arithmetic  249 us (26%)
  matrix products  92.9 us (10%)
  local copies, waits for them, and re-layouts  37.6 us (4%)
  blocking collectives  23.9 us (2%)
  between operations  20.4 us (2%)
    psum x4, waiting for transfers between devices, broadcast(): return lax.psum(block, axis)  232 us
    another operation x29, other arithmetic, on_device(): factor = jnp.linalg.cholesky(diag_block)  158 us
    all_gather x1, waiting for transfers between devices, on_device(): every_sample = lax.all_gather(centered, 'row', axis=0, tiled=True)  147 us
    all_to_all x1, waiting for transfers between devices, on_device(): lax.all_to_all(every_sample, 'col', split_axis=0, concat_axis=1, tiled=True)  127 us
    another operation x5, other arithmetic, on_device(): lax.linalg.triangular_solve(factor, column, left_side=False, lower=True,...  79.4 us
    all_gather x1, waiting for transfers between devices, on_device(): own_rows = lax.all_gather(centered, 'col', axis=1, tiled=True)  32.8 us
    dot_general x2, matrix products, jacobian(): jnp.dot(embedded, weights[panel_index], precision=lax.Precision.HIGHEST,...  19.7 us
  transfers between devices with their start and end apart: 7, of which 7 were waited for; matrix products, arithmetic and copies ran while one was open for 1% of the time, Pallas kernels for 0%

commit v1 on v0

v1 whole, which is shorter than its diff:
```python
import functools
import math

import jax
import jax.numpy as jnp
from jax import lax
from jax.experimental import pallas as pl
from jax.experimental.pallas import tpu as pltpu
from jax.sharding import PartitionSpec as P

norm_eps = 1e-06
diag_shift = 0.05
BLOCK = 128
BF = jnp.bfloat16
F32 = jnp.float32


def split3(x):
    terms = []
    for _ in range(3):
        hi = lax.reduce_precision(x, 8, 7)
        terms.append(hi.astype(BF))
        x = x - hi
    return terms


def split2(x):
    hi = x.astype(BF)
    return hi, (x - hi.astype(F32)).astype(BF)


def dot3(a, b, dims):
    (ah, al), (bh, bl) = a, b
    d = functools.partial(
        lax.dot_general, dimension_numbers=(dims, ((), ())), preferred_element_type=F32
    )
    return d(ah, bh) + (d(ah, bl) + d(al, bh))


def inverse_factor(block):
    tiles = BLOCK // 8
    row = lax.broadcasted_iota(jnp.int32, (8, BLOCK), 0)
    lane = lax.broadcasted_iota(jnp.int32, (8, BLOCK), 1)
    d = [block[8 * t : 8 * t + 8] for t in range(tiles)]
    m = [(lane == row + 8 * t).astype(F32) for t in range(tiles)]
    for j in range(BLOCK):
        t0, s = divmod(j, 8)
        drow = jnp.broadcast_to(d[t0][s : s + 1], (8, BLOCK))
        mrow = jnp.broadcast_to(m[t0][s : s + 1], (8, BLOCK))
        inv = 1.0 / jnp.broadcast_to(drow[:, j : j + 1], (8, BLOCK))
        dn = drow * inv
        mn = mrow * inv
        for t in range(t0, tiles):
            if t == t0 and s == 7:
                continue
            f = jnp.broadcast_to(d[t][:, j : j + 1], (8, BLOCK))
            if t == t0:
                f = jnp.where(row > s, f, 0.0)
            d[t] = d[t] - f * dn
            m[t] = m[t] - f * mn
    out = []
    for t in range(tiles):
        piv = jnp.sum(jnp.where(lane == row + 8 * t, d[t], 0.0), axis=1, keepdims=True)
        out.append(m[t] * lax.rsqrt(piv))
    return jnp.concatenate(out, axis=0)


def eliminate_kernel(x_ref, w_ref, u_hi, u_lo, work):
    n, width = x_ref.shape
    steps = n // BLOCK

    def step(k, carry):
        rows = pl.ds(pl.multiple_of(k * BLOCK, BLOCK), BLOCK)
        work[...] = x_ref[rows, :]
        for case in range(1, steps):

            @pl.when(k == case)
            def _():
                done = case * BLOCK
                left = (u_hi[:done, done : done + BLOCK], u_lo[:done, done : done + BLOCK])
                right = (u_hi[:done, done:], u_lo[:done, done:])
                work[:, done:] = work[:, done:] - dot3(left, right, ((0,), (0,)))

        inverse = split2(inverse_factor(work[:, rows]))
        solved = dot3(inverse, split2(work[...]), ((1,), (0,)))
        hi, lo = split2(solved)
        u_hi[rows, :] = hi
        u_lo[rows, :] = lo
        w_ref[rows, :] = solved[:, n:]
        return carry

    lax.fori_loop(0, steps, step, 0)


def eliminate(x):
    n, width = x.shape
    return pl.pallas_call(
        eliminate_kernel,
        out_shape=jax.ShapeDtypeStruct((n, width - n), F32),
        in_specs=[pl.BlockSpec(memory_space=pltpu.VMEM)],
        out_specs=pl.BlockSpec(memory_space=pltpu.VMEM),
        scratch_shapes=[
            pltpu.VMEM((n, width), BF),
            pltpu.VMEM((n, width), BF),
            pltpu.VMEM((BLOCK, width), F32),
        ],
        compiler_params=pltpu.CompilerParams(vmem_limit_bytes=56 * 1024 * 1024),
    )(x)


def on_device(occupations, table, weights, biases, heads, energies):
    row_count, orb = occupations.shape
    row_devices = lax.axis_size("row")
    col_devices = lax.axis_size("col")
    row_index = lax.axis_index("row")
    col_index = lax.axis_index("col")
    total = row_count * row_devices
    width = total // col_devices
    head_count = 2 * width
    hp = lax.Precision.HIGHEST

    occ = lax.all_gather(occupations.astype(BF), "row", axis=0, tiled=True)
    start = jnp.where(lax.iota(jnp.int32, row_devices) == row_index, energies[:, None], 0.0)
    rhs_all = lax.psum(start.T.reshape(-1), "row")

    level0 = table[:orb]
    steps = jnp.concatenate([table[orb : 2 * orb] - level0, table[2 * orb :] - level0], axis=0)
    base = jnp.sum(level0, axis=0)
    both = jnp.concatenate([steps, base[None]], axis=0)
    w = jnp.concatenate([weights[0], weights[1]], axis=1)
    folded = jnp.dot(both, w, precision=hp, preferred_element_type=F32)
    t_steps = jnp.concatenate(split3(folded[: 2 * orb])[:2], axis=0)
    t_base = folded[2 * orb]
    half_bias = 0.5 * biases.reshape(-1)
    gram = jnp.dot(both, both.T, precision=hp, preferred_element_type=F32)

    x = jnp.concatenate([(occ == 1).astype(BF), (occ == 2).astype(BF)], axis=1)
    x2 = jnp.concatenate([x, x], axis=1)
    g = gram[: 2 * orb, : 2 * orb]
    g_hi, g_lo, _ = split3(g)
    xg = jnp.dot(x, g_hi, preferred_element_type=F32) + jnp.dot(x, g_lo, preferred_element_type=F32)
    square = jnp.sum((xg + 2.0 * gram[2 * orb, : 2 * orb]) * x.astype(F32), axis=1)
    square = square + gram[2 * orb, 2 * orb]
    half_scale = 0.5 * lax.rsqrt(jnp.maximum(square, 0.0) / table.shape[1] + norm_eps)

    def gates(rows, scale, t, t0, b):
        return jnp.tanh(
            scale[:, None] * (jnp.dot(rows, t, preferred_element_type=F32) + t0) + b
        )

    mean = jnp.sum(gates(x2, half_scale, t_steps, t_base, half_bias), axis=0) / total
    consts = jnp.stack([t_base, half_bias, heads.reshape(-1) * (0.5 / math.sqrt(total)), mean])
    c1, c2, c3 = split3(consts)
    pack = jnp.concatenate([t_steps, c1, c2, c3, jnp.zeros_like(c1)], axis=0)
    pack = lax.all_gather(pack, "col", axis=1, tiled=True)
    t_all = pack[: 4 * orb]
    tail = pack[4 * orb :].astype(F32)
    t_base, half_bias, amp, mean = tail[0:4] + (tail[4:8] + tail[8:12])

    def pick(a, axis=0):
        return jnp.concatenate(
            [
                lax.slice_in_dim(a, 0, head_count, axis=axis),
                lax.dynamic_slice_in_dim(a, row_index * row_count, row_count, axis),
                lax.dynamic_slice_in_dim(a, col_index * width, width, axis),
            ],
            axis=axis,
        )

    centered = (
        amp * (gates(pick(x2), pick(half_scale), t_all, t_base, half_bias) - mean)
    ).astype(BF)
    ids = pick(lax.iota(jnp.int32, total))

    def gram_of(a, b, a_ids, b_ids):
        k = lax.dot_general(a, b, (((1,), (1,)), ((), ())), preferred_element_type=F32)
        return k + jnp.where(a_ids[:, None] == b_ids[None, :], diag_shift, 0.0)

    top = gram_of(centered[:head_count], centered, ids[:head_count], ids)
    mid = head_count + row_count
    own = gram_of(centered[head_count:mid], centered[mid:], ids[head_count:mid], ids[mid:])
    side = jnp.pad(rhs_all[:head_count, None], ((0, 0), (0, BLOCK - 1)))
    solved = eliminate(jnp.concatenate([top, side], axis=1))
    update = lax.dot_general(
        solved[:, :row_count],
        solved[:, row_count:],
        (((0,), (0,)), ((), ())),
        precision=lax.Precision.HIGH,
        preferred_element_type=F32,
    )
    schur = own - update[:, :width]
    front = solved[:, row_count + width]
    front = jnp.pad(front, (0, total - head_count))
    front = lax.dynamic_slice_in_dim(front, row_index * row_count, row_count)
    rest = energies - update[:, width]
    own_ids = ids[head_count:mid]
    return (schur, jnp.where(own_ids < head_count, front, rest))


def solution(mesh):
    placed = (P("row", None), P(), P(None, None, "col"), P(None, "col"), P(None, "col"), P("row"))
    return jax.shard_map(
        on_device,
        mesh=mesh,
        in_specs=placed,
        out_specs=(P("row", "col"), P("row")),
        check_vma=False,
    )
```

time: 975 us -> 409 us (0.42)
  waiting for transfers between devices: 539 us -> 54.9 us
  other arithmetic: 249 us -> 14.1 us
  Pallas kernels: 0 us -> 158 us
  matrix products: 92.9 us -> 129 us
  local copies, waits for them, and re-layouts: 37.6 us -> 12.7 us
    another operation x36 -> x0, other arithmetic: 238 us -> none  [the longest x29 158 us: on_device(): factor = jnp.linalg.cholesky(diag_block)]
    psum x4 -> x0, waiting for transfers between devices: 232 us -> none  [broadcast(): return lax.psum(block, axis)]
    pallas_call x0 -> x1, Pallas kernels: none -> 158 us  [eliminate(): pl.pallas_call(eliminate_kernel, out_shape=jax.ShapeDtypeStruct((n, width...]
    all_to_all x1 -> x0, waiting for transfers between devices: 127 us -> none  [on_device(): lax.all_to_all(every_sample, 'col', split_axis=0, concat_axis=1, tiled=True)]
    all_gather x2, waiting for transfers between devices: 180 us -> 54.9 us  [the longest x1 35.8 us: on_device(): pack = lax.all_gather(pack, 'col', axis=1, tiled=True)]
    dot_general x8 -> x9, matrix products: 53.4 us -> 129 us  [the longest x2 65.8 us: gram_of(): lax.dot_general(a, b, (((1,), (1,)), ((), ())), preferred_element_type=F32)]
    another operation x54 -> x0, matrix products: 39.5 us -> none  [the longest x14 16.2 us: on_device(): lax.linalg.triangular_solve(factor, column, left_side=False, lower=True,...]
    another operation x35 -> x1, local copies, waits for them, and re-layouts: 16.2 us -> 0.09 us  [on_device(): t_base, half_bias, amp, mean = tail[0:4] + (tail[4:8] + tail[8:12])]
  transfers between devices with their start and end apart: 7 -> 2, of which waited for: 7 -> 2; matrix products, arithmetic and copies ran while one was open for 1% -> 3% of each run, Pallas kernels for 0% -> 0%
where the time goes in v1:
time: 409 us; the launch traced here: 402 us
  Pallas kernels  158 us (39%)
  matrix products  129 us (32%)
  waiting for transfers between devices  54.9 us (13%)
  blocking collectives  17.4 us (4%)
  between operations  14.8 us (4%)
  other arithmetic  14.1 us (3%)
  local copies, waits for them, and re-layouts  12.7 us (3%)
    pallas_call x1, Pallas kernels, eliminate(): pl.pallas_call(eliminate_kernel, out_shape=jax.ShapeDtypeStruct((n, width...  158 us
    dot_general x2, matrix products, gram_of(): lax.dot_general(a, b, (((1,), (1,)), ((), ())), preferred_element_type=F32)  65.8 us
    dot_general x2, matrix products, gates(): jnp.dot(rows, t, preferred_element_type=F32) + t0  48.6 us
    all_gather x1, waiting for transfers between devices, on_device(): pack = lax.all_gather(pack, 'col', axis=1, tiled=True)  35.8 us
    all_gather x1, waiting for transfers between devices, on_device(): occ = lax.all_gather(occupations.astype(BF), 'row', axis=0, tiled=True)  19.1 us
    psum x1, blocking collectives, on_device(): rhs_all = lax.psum(start.T.reshape(-1), 'row')  17.4 us
  transfers between devices with their start and end apart: 2, of which 2 were waited for; matrix products, arithmetic and copies ran while one was open for 3% of the time, Pallas kernels for 0%

profile of v1, /device:TPU:0, one launch (start us, length us, event | category | flops | bytes accessed | tf_op | source)
XLA Modules:
  0.0 401.7 jit_solution(3086241352482334577)
XLA Ops:
  7.2 1.2 copy.10
  8.5 0.7 convert_element_type.45
  9.3 0.8 multiply_bitcast_fusion
  10.1 0.9 multiply_bitcast_fusion.2
  12.2 1.5 slice_subtract_fusion.1
  13.7 1.9 fusion.33
  16.6 3.8 fusion.12
  21.8 19.1 %all-gather.3.cloned.1.call-done = bf16[4096,128]{0,1:T(8,128)(2,1)} async-done(((bf16[1024,128]{0,1:T(8,128)(2,1)}), bf16[4096,128]{0,1:T(8,128)(2,1)}) %all-gather.3.cloned.1.call-update) | async-done | bytes 1048592 | tf_op jit(solution)/shard_map/all_gather | solution.py:122
  40.9 1.7 compare_convert_fusion.1
  42.6 0.8 fusion.27
  43.4 1.2 fusion.22
  45.3 6.3 %tanh_reduce_fusion = f32[1024]{0:T(1024)S(1)} fusion(f32[1024]{0:T(1024)S(1)} %bitcast.46, f32[1024]{0:T(1024)S(1)} %bitcast.41, f32[4096]{0:T(1024)S(1)} %rsqrt_multiply_fusion, bf16[256,1024]{1,0:T(8,128)(2,1)S(1)} %get-tuple-element.9, bf16[256,1024]{1,0:T(8,128)(2,1)S(1)} %get-tuple-element.10, bf16[4096,128]{0,1:T(8,128)(2,1)S(1)} %get-tuple-element.12, ...), kind=kOutput, calls=%fused_computation.5 | convolution fusion | flops 4330617856 | bytes 3174400 | tf_op jit(solution)/shard_map/dot_general | solution.py:148
  51.7 4.1 %concatenate.37 = bf16[528,1024]{1,0:T(8,128)(2,1)} concatenate(bf16[256,1024]{1,0:T(8,128)(2,1)S(1)} %get-tuple-element.10, bf16[256,1024]{1,0:T(8,128)(2,1)S(1)} %get-tuple-element.9, bf16[4,1024]{1,0:T(4,128)(2,1)S(1)} %get-tuple-element.21, bf16[4,1024]{1,0:T(4,128)(2,1)S(1)} %get-tuple-element.20, bf16[4,1024]{1,0:T(4,128)(2,1)S(1)} %get-tuple-element.19, ...), dimensions={0} | concatenate | bytes 2162688 | tf_op jit(solution)/shard_map/concatenate | solution.py:154
  55.9 17.4 %psum.7 = f32[4096]{0:T(1024)S(1)} all-reduce(f32[4096]{0:T(1024)S(1)} %bitcast.33), channel_id=1, replica_groups=mesh['row'=4,'col'=8] {'row'}, use_global_device_ids=true, to_apply=%region_3.4 | all-reduce | flops 4096 | bytes 32768 | tf_op jit(solution)/shard_map/psum | solution.py:124
  74.9 35.8 %all-gather.5.cloned.1.call-done = bf16[528,8192]{1,0:T(8,128)(2,1)} async-done(((bf16[528,1024]{1,0:T(8,128)(2,1)}), bf16[528,8192]{1,0:T(8,128)(2,1)}) %all-gather.5.cloned.1.call-update) | async-done | bytes 8650768 | tf_op jit(solution)/shard_map/all_gather | solution.py:155
  110.7 1.0 slice_convert_fusion
  111.9 42.3 %multiply_convert_fusion = bf16[2560,8192]{1,0:T(8,128)(2,1)} fusion(f32[8192]{0:T(1024)S(1)} %bitcast.35, f32[8192]{0:T(1024)S(1)} %bitcast.36, f32[8192]{0:T(1024)S(1)} %bitcast.37, f32[2560]{0:T(1024)S(1)} %pad_maximum_fusion.8, f32[8192]{0:T(1024)S(1)} %bitcast.34, bf16[528,8192]{1,0:T(8,128)(2,1)} %all-gather.5.cloned.1.call-done, ...), kind=kOutput, calls=%fused_computation | convolution fusion | flops 21608529920 | bytes 53094400 | tf_op jit(solution)/shard_map/dot_general | solution.py:148
  154.1 49.7 %select_add_fusion = f32[1024,2560]{1,0:T(8,128)S(1)} fusion(bf16[2560,8192]{1,0:T(8,128)(2,1)} %multiply_convert_fusion, s32[2560]{0:T(1024)S(1)} %pad_add_fusion, s32[1024]{0:T(1024)S(1)} %iota_add_fusion), kind=kOutput, calls=%fused_computation.8 | convolution fusion | flops 42957537280 | bytes 69220352 | tf_op jit(solution)/shard_map/dot_general | solution.py:176
  203.8 4.9 %select_maximum_fusion.x_ref = f32[1024,2688]{1,0:T(8,128)} fusion(f32[1024,1]{1,0:T(8,128)S(1)} %copy.11, f32[1024,2560]{1,0:T(8,128)S(1)} %select_add_fusion), kind=kLoop, calls=%fused_computation.6 | loop fusion | flops 8257536 | bytes 21499904 | tf_op jit(solution)/shard_map/concatenate | solution.py:183
  208.7 158.2 %shard_map.77 = f32[1024,1664]{1,0:T(8,128)} custom-call(f32[1024,2688]{1,0:T(8,128)} %select_maximum_fusion.x_ref), custom_call_target="tpu_custom_call" | custom-call | tf_op jit(solution)/shard_map/pallas_call | solution.py:97
  366.9 1.2 slice_reduce_fusion
  368.2 7.3 %fusion.10 = f32[1024,640]{0,1:T(8,128)S(1)} fusion(f32[1024,1664]{1,0:T(8,128)} %shard_map.77), kind=kOutput, calls=%fused_computation.14 | convolution fusion | flops 4026531840 | bytes 9437184 | tf_op jit(solution)/shard_map/dot_general | solution.py:184
  375.8 1.8 copy.13
  377.6 16.2 %add_subtract_fusion = f32[1024,512]{1,0:T(8,128)} fusion(f32[1024,512]{1,0:T(8,128)} %copy.13, bf16[2560,8192]{1,0:T(8,128)(2,1)} %multiply_convert_fusion, s32[512]{0:T(512)S(1)} %copy-done.8, s32[1024]{0:T(1024)S(1)} %copy-done.6), kind=kOutput, calls=%fused_computation.28 | convolution fusion | flops 8592031744 | bytes 29366272 | tf_op jit(solution)/shard_map/dot_general | solution.py:176
  (58 shorter events, 7.0 us)
Async XLA Ops:
  7.2 33.7 %all-gather.3.cloned.1.call-start = ((), (), s32[]{:S(2)}) async-start(), calls=%async_computation | async-start | bytes 1310720 | tf_op jit(solution)/shard_map/all_gather | solution.py:122
  9.2 101.5 %all-gather.5.cloned.1.call-start = ((), (), s32[]{:S(2)}) async-start(), calls=%async_computation.1 | async-start | bytes 9732096 | tf_op jit(solution)/shard_map/all_gather | solution.py:155
  9.3 6.9 %copy-start = (f32[2,1024,512]{2,1,0:T(8,128)S(1)}, f32[2,1024,512]{2,1,0:T(8,128)}, u32[]{:S(2)}) copy-start(f32[2,1024,512]{2,1,0:T(8,128)} %param.8) | copy-start | bytes 12582916
  42.6 0.8 copy-start.10
  43.3 2.0 copy-start.2
  43.3 2.0 copy-start.9
  45.3 6.3 %copy-start.1 = (f32[1,1,2,512]{3,1,2,0:T(1,128)S(1)}, f32[1,1,2,512]{3,1,2,0:T(1,128)}, u32[]{:S(2)}) copy-start(f32[1,1,2,512]{3,1,2,0:T(1,128)} %copy.14) | copy-start | bytes 12292
  45.3 10.5 %copy-start.3 = (f32[1024]{0:T(1024)S(1)}, f32[1024]{0:T(1024)}, u32[]{:S(2)}) copy-start(f32[1024]{0:T(1024)} %param.11) | copy-start | bytes 12292
  73.6 0.6 copy-start.7
  73.7 0.6 copy-start.5
  375.5 2.1 copy-start.6
  375.6 2.1 copy-start.8
  377.6 16.2 %copy-start.4 = (f32[1024]{0:T(1024)S(1)}, f32[1024]{0:T(1024)}, u32[]{:S(2)}) copy-start(f32[1024]{0:T(1024)} %param.11) | copy-start | bytes 12292
Sparse Core Ops, SparseCore 0:
  10.1 30.6 all-gather.2
  56.0 54.7 all-gather.4

commit v2 on v1

--- a/solution.py
+++ b/solution.py
@@ -43,30 +43,63 @@
     lane = lax.broadcasted_iota(jnp.int32, (8, BLOCK), 1)
     d = [block[8 * t : 8 * t + 8] for t in range(tiles)]
     m = [(lane == row + 8 * t).astype(F32) for t in range(tiles)]
-    for j in range(BLOCK):
+    out = [jnp.zeros((8, BLOCK), F32) for _ in range(tiles)]
+
+    def full(x):
+        return jnp.broadcast_to(x, (8, BLOCK))
+
+    for j in range(0, BLOCK, 4):
         t0, s = divmod(j, 8)
-        drow = jnp.broadcast_to(d[t0][s : s + 1], (8, BLOCK))
-        mrow = jnp.broadcast_to(m[t0][s : s + 1], (8, BLOCK))
-        inv = 1.0 / jnp.broadcast_to(drow[:, j : j + 1], (8, BLOCK))
-        dn = drow * inv
-        mn = mrow * inv
+        d0, d1, d2, d3 = [full(d[t0][s + i : s + i + 1]) for i in range(4)]
+        m0, m1, m2, m3 = [full(m[t0][s + i : s + i + 1]) for i in range(4)]
+        a, b, e0, h0 = [full(d0[:, j + i : j + i + 1]) for i in range(4)]
+        c, e1, h1 = [full(d1[:, j + i : j + i + 1]) for i in range(1, 4)]
+        r, u = [full(d2[:, j + i : j + i + 1]) for i in range(2, 4)]
+        v = full(d3[:, j + 3 : j + 4])
+
+        inv = 1.0 / (a * c - b * b)
+        ai, bi, ci = a * inv, b * inv, c * inv
+        alpha2, beta2 = ci * e0 - bi * e1, ai * e1 - bi * e0
+        alpha3, beta3 = ci * h0 - bi * h1, ai * h1 - bi * h0
+        r = r - (e0 * alpha2 + e1 * beta2)
+        u = u - (e0 * alpha3 + e1 * beta3)
+        v = v - (h0 * alpha3 + h1 * beta3)
+        inv2 = 1.0 / (r * v - u * u)
+        ri, ui, vi = r * inv2, u * inv2, v * inv2
+
+        q0, q1 = ci * d0 - bi * d1, ai * d1 - bi * d0
+        p0, p1 = ci * m0 - bi * m1, ai * m1 - bi * m0
+        d2, d3 = d2 - (e0 * q0 + e1 * q1), d3 - (h0 * q0 + h1 * q1)
+        m2, m3 = m2 - (e0 * p0 + e1 * p1), m3 - (h0 * p0 + h1 * p1)
+        q2, q3 = vi * d2 - ui * d3, ri * d3 - ui * d2
+        p2, p3 = vi * m2 - ui * m3, ri * m3 - ui * m2
+
+        ba, ur = b / a, u / r
+        done = (
+            m0 * lax.rsqrt(a),
+            (m1 - ba * m0) * lax.rsqrt(c - ba * b),
+            m2 * lax.rsqrt(r),
+            (m3 - ur * m2) * lax.rsqrt(v - ur * u),
+        )
+        for i in range(4):
+            out[t0] = jnp.where(row == s + i, done[i], out[t0])
+
         for t in range(t0, tiles):
-            if t == t0 and s == 7:
+            if t == t0 and s == 4:
                 continue
-            f = jnp.broadcast_to(d[t][:, j : j + 1], (8, BLOCK))
+            f0, f1, f2, f3 = [full(d[t][:, j + i : j + i + 1]) for i in range(4)]
+            f2 = f2 - (f0 * alpha2 + f1 * beta2)
+            f3 = f3 - (f0 * alpha3 + f1 * beta3)
             if t == t0:
-                f = jnp.where(row > s, f, 0.0)
-            d[t] = d[t] - f * dn
-            m[t] = m[t] - f * mn
-    out = []
-    for t in range(tiles):
-        piv = jnp.sum(jnp.where(lane == row + 8 * t, d[t], 0.0), axis=1, keepdims=True)
-        out.append(m[t] * lax.rsqrt(piv))
+                f0, f1, f2, f3 = [jnp.where(row > 3, f, 0.0) for f in (f0, f1, f2, f3)]
+            d[t] = d[t] - ((f0 * q0 + f1 * q1) + (f2 * q2 + f3 * q3))
+            m[t] = m[t] - ((f0 * p0 + f1 * p1) + (f2 * p2 + f3 * p3))
     return jnp.concatenate(out, axis=0)
 
 
-def eliminate_kernel(x_ref, w_ref, u_hi, u_lo, work):
+def eliminate_kernel(x_ref, update_ref, side_ref, u_hi, u_lo, work):
     n, width = x_ref.shape
+    row_count = update_ref.shape[0]
     steps = n // BLOCK
 
     def step(k, carry):
@@ -86,19 +119,35 @@
         hi, lo = split2(solved)
         u_hi[rows, :] = hi
         u_lo[rows, :] = lo
-        w_ref[rows, :] = solved[:, n:]
+        side_ref[rows, :] = solved[:, width - BLOCK :]
         return carry
 
     lax.fori_loop(0, steps, step, 0)
 
-
-def eliminate(x):
+    def product(i, carry):
+        cols = pl.ds(pl.multiple_of(n + i * BLOCK, BLOCK), BLOCK)
+        rows = pl.ds(pl.multiple_of(i * BLOCK, BLOCK), BLOCK)
+        left = (u_hi[:, cols], u_lo[:, cols])
+        right = (u_hi[:, n + row_count :], u_lo[:, n + row_count :])
+        update_ref[rows, :] = dot3(left, right, ((0,), (0,)))
+        return carry
+
+    lax.fori_loop(0, row_count // BLOCK, product, 0)
+
+
+def eliminate(x, row_count):
     n, width = x.shape
     return pl.pallas_call(
         eliminate_kernel,
-        out_shape=jax.ShapeDtypeStruct((n, width - n), F32),
+        out_shape=(
+            jax.ShapeDtypeStruct((row_count, width - n - row_count), F32),
+            jax.ShapeDtypeStruct((n, BLOCK), F32),
+        ),
         in_specs=[pl.BlockSpec(memory_space=pltpu.VMEM)],
-        out_specs=pl.BlockSpec(memory_space=pltpu.VMEM),
+        out_specs=(
+            pl.BlockSpec(memory_space=pltpu.VMEM),
+            pl.BlockSpec(memory_space=pltpu.VMEM),
+        ),
         scratch_shapes=[
             pltpu.VMEM((n, width), BF),
             pltpu.VMEM((n, width), BF),
@@ -119,9 +168,12 @@
     head_count = 2 * width
     hp = lax.Precision.HIGHEST
 
-    occ = lax.all_gather(occupations.astype(BF), "row", axis=0, tiled=True)
-    start = jnp.where(lax.iota(jnp.int32, row_devices) == row_index, energies[:, None], 0.0)
-    rhs_all = lax.psum(start.T.reshape(-1), "row")
+    terms = jnp.concatenate([e.reshape(-1, orb) for e in split3(energies)], axis=0)
+    sent = jnp.concatenate([occupations.astype(BF), terms], axis=0)
+    came = lax.all_gather(sent, "row", axis=0)
+    occ = came[:, :row_count].reshape(total, orb)
+    terms = came[:, row_count:].astype(F32).reshape(row_devices, 3, row_count)
+    rhs_all = (terms[:, 0] + (terms[:, 1] + terms[:, 2])).reshape(total)
 
     level0 = table[:orb]
     steps = jnp.concatenate([table[orb : 2 * orb] - level0, table[2 * orb :] - level0], axis=0)
@@ -180,16 +232,9 @@
     mid = head_count + row_count
     own = gram_of(centered[head_count:mid], centered[mid:], ids[head_count:mid], ids[mid:])
     side = jnp.pad(rhs_all[:head_count, None], ((0, 0), (0, BLOCK - 1)))
-    solved = eliminate(jnp.concatenate([top, side], axis=1))
-    update = lax.dot_general(
-        solved[:, :row_count],
-        solved[:, row_count:],
-        (((0,), (0,)), ((), ())),
-        precision=lax.Precision.HIGH,
-        preferred_element_type=F32,
-    )
+    update, side = eliminate(jnp.concatenate([top, side], axis=1), row_count)
     schur = own - update[:, :width]
-    front = solved[:, row_count + width]
+    front = side[:, 0]
     front = jnp.pad(front, (0, total - head_count))
     front = lax.dynamic_slice_in_dim(front, row_index * row_count, row_count)
     rest = energies - update[:, width]

time: 409 us -> 319 us (0.78); the launches traced: 402 us -> 319 us
  Pallas kernels: 158 us -> 71.2 us
  blocking collectives: 17.4 us -> 0 us
  waiting for transfers between devices: 54.9 us -> 70.9 us
  matrix products: 129 us -> 135 us
    pallas_call x1, Pallas kernels: 158 us -> 71.2 us  [eliminate(): pl.pallas_call(eliminate_kernel, out_shape=(jax.ShapeDtypeStruct((row_cou...]
    psum x1 -> x0, blocking collectives: 17.4 us -> none  [on_device(): rhs_all = lax.psum(start.T.reshape(-1), 'row')]
    all_gather x1, waiting for transfers between devices: 35.8 us -> 53 us  [on_device(): pack = lax.all_gather(pack, 'col', axis=1, tiled=True)]
    dot_general x2, matrix products: 65.8 us -> 78.3 us  [gram_of(): lax.dot_general(a, b, (((1,), (1,)), ((), ())), preferred_element_type=F32)]
    dot_general x1 -> x0, matrix products: 7.35 us -> none  [on_device(): lax.dot_general(solved[:, :row_count], solved[:, row_count:], (((0,), (0,...]
  transfers between devices with their start and end apart: 2 -> 2, of which waited for: 2 -> 2; matrix products, arithmetic and copies ran while one was open for 3% -> 5% of each run, Pallas kernels for 0% -> 0%
where the time goes in v2:
time: 319 us
  matrix products  135 us (42%)
  Pallas kernels  71.2 us (22%)
  waiting for transfers between devices  70.9 us (22%)
  other arithmetic  17.3 us (5%)
  between operations  14.6 us (5%)
  local copies, waits for them, and re-layouts  10.5 us (3%)
    dot_general x2, matrix products, gram_of(): lax.dot_general(a, b, (((1,), (1,)), ((), ())), preferred_element_type=F32)  78.3 us
    pallas_call x1, Pallas kernels, eliminate(): pl.pallas_call(eliminate_kernel, out_shape=(jax.ShapeDtypeStruct((row_cou...  71.2 us
    all_gather x1, waiting for transfers between devices, on_device(): pack = lax.all_gather(pack, 'col', axis=1, tiled=True)  53 us
    dot_general x2, matrix products, gates(): jnp.dot(rows, t, preferred_element_type=F32) + t0  48.6 us
    all_gather x1, waiting for transfers between devices, on_device(): came = lax.all_gather(sent, 'row', axis=0)  17.8 us
  transfers between devices with their start and end apart: 2, of which 2 were waited for; matrix products, arithmetic and copies ran while one was open for 5% of the time, Pallas kernels for 0%

profile of v2, /device:TPU:0, one launch (start us, length us, event | category | flops | bytes accessed | tf_op | source)
XLA Modules:
  0.0 319.1 jit_solution(11069576134875793497)
XLA Ops:
  7.9 1.1 convert_element_type.61
  9.0 0.7 pad_maximum_fusion.7
  9.8 0.8 multiply_bitcast_fusion
  10.6 0.9 multiply_bitcast_fusion.2
  12.7 1.5 slice_subtract_fusion.2
  14.2 1.9 fusion.30
  17.1 3.8 %fusion.10 = f32[257,1024]{1,0:T(8,128)S(1)} fusion(f32[1024,512]{1,0:T(8,128)S(1)} %get-tuple-element.9, f32[1024,512]{1,0:T(8,128)S(1)} %get-tuple-element.8, f32[1,1024]{1,0:T(1,128)S(1)} %bitcast.50, f32[128,1024]{1,0:T(8,128)S(1)} %get-tuple-element.11, f32[128,1024]{1,0:T(8,128)S(1)} %get-tuple-element.10), kind=kOutput, calls=%fused_computation.14 | convolution fusion | flops 3235383296 | bytes 6299648 | tf_op jit(solution)/shard_map/dot_general | solution.py:183
  22.0 1.2 fusion.26
  23.2 17.8 %all-gather.6.cloned.1.call-done = bf16[4192,128]{1,0:T(8,128)(2,1)} async-done(((bf16[1048,128]{1,0:T(8,128)(2,1)}), bf16[4192,128]{1,0:T(8,128)(2,1)}) %all-gather.6.cloned.1.call-update) | async-done | bytes 1073168 | tf_op jit(solution)/shard_map/all_gather | solution.py:173
  41.0 1.7 compare_convert_fusion.1
  42.7 0.8 copy.12
  44.1 0.8 fusion.24
  44.9 1.2 fusion.19
  46.8 6.3 %tanh_reduce_fusion = f32[1024]{0:T(1024)S(1)} fusion(f32[1024]{0:T(1024)S(1)} %bitcast.51, f32[1024]{0:T(1024)S(1)} %bitcast.47, f32[4096]{0:T(1024)S(1)} %rsqrt_multiply_fusion, bf16[256,1024]{1,0:T(8,128)(2,1)S(1)} %copy-done.1, bf16[256,1024]{1,0:T(8,128)(2,1)S(1)} %copy-done.2, bf16[4096,128]{0,1:T(8,128)(2,1)S(1)} %copy.13, bf16[4096,128]{0,1:T(8,128)(2,1)S(1)} %copy.12), kind=kOutput, calls=%fused_computation.5 | convolution fusion | flops 4330617856 | bytes 3174400 | tf_op jit(solution)/shard_map/dot_general | solution.py:200
  53.2 4.1 %concatenate.41 = bf16[528,1024]{1,0:T(8,128)(2,1)} concatenate(bf16[256,1024]{1,0:T(8,128)(2,1)S(1)} %copy-done.2, bf16[256,1024]{1,0:T(8,128)(2,1)S(1)} %copy-done.1, bf16[4,1024]{1,0:T(4,128)(2,1)S(1)} %get-tuple-element.28, bf16[4,1024]{1,0:T(4,128)(2,1)S(1)} %get-tuple-element.27, bf16[4,1024]{1,0:T(4,128)(2,1)S(1)} %get-tuple-element.26, bf16[4,1024]{1,0:T(4,128)(2,1)S(1)} %broadcast_in_dim.34), dimensions={0} | concatenate | bytes 2162688 | tf_op jit(solution)/shard_map/concatenate | solution.py:206
  57.4 0.7 slice_convert_fusion.1
  59.1 53.0 %all-gather.4.cloned.1.call-done = bf16[528,8192]{1,0:T(8,128)(2,1)} async-done(((bf16[528,1024]{1,0:T(8,128)(2,1)}), bf16[528,8192]{1,0:T(8,128)(2,1)}) %all-gather.4.cloned.1.call-update) | async-done | bytes 8650768 | tf_op jit(solution)/shard_map/all_gather | solution.py:207
  112.2 1.0 slice_convert_fusion
  113.3 42.3 %multiply_convert_fusion = bf16[2560,8192]{1,0:T(8,128)(2,1)} fusion(f32[8192]{0:T(1024)S(1)} %bitcast.42, f32[8192]{0:T(1024)S(1)} %bitcast.43, f32[8192]{0:T(1024)S(1)} %bitcast.44, f32[2560]{0:T(1024)S(1)} %pad_maximum_fusion.9, f32[8192]{0:T(1024)S(1)} %bitcast.41, bf16[528,8192]{1,0:T(8,128)(2,1)} %all-gather.4.cloned.1.call-done, ...), kind=kOutput, calls=%fused_computation | convolution fusion | flops 21608529920 | bytes 53094400 | tf_op jit(solution)/shard_map/dot_general | solution.py:200
  155.6 62.0 %select_add_fusion = f32[1024,2560]{1,0:T(8,128)S(1)} fusion(bf16[2560,8192]{1,0:T(8,128)(2,1)} %multiply_convert_fusion, s32[2560]{0:T(1024)S(1)} %pad_add_fusion, s32[1024]{0:T(1024)S(1)} %get-tuple-element.34), kind=kOutput, calls=%fused_computation.8 | convolution fusion | flops 42957537280 | bytes 69220352 | tf_op jit(solution)/shard_map/dot_general | solution.py:228
  217.6 4.9 %select_maximum_fusion.x_ref = f32[1024,2688]{1,0:T(8,128)} fusion(f32[1024,1]{1,0:T(8,128)S(1)} %copy.11, f32[1024,2560]{1,0:T(8,128)S(1)} %select_add_fusion), kind=kLoop, calls=%fused_computation.6 | loop fusion | flops 8257536 | bytes 21499904 | tf_op jit(solution)/shard_map/concatenate | solution.py:235
  222.4 71.2 %shard_map.77 = (f32[1024,640]{1,0:T(8,128)}, f32[1024,128]{1,0:T(8,128)}) custom-call(f32[1024,2688]{1,0:T(8,128)} %select_maximum_fusion.x_ref), custom_call_target="tpu_custom_call" | custom-call | tf_op jit(solution)/shard_map/pallas_call | solution.py:140
  293.6 16.4 %slice_subtract_fusion = f32[1024,512]{1,0:T(8,128)} fusion(f32[1024,640]{1,0:T(8,128)} %get-tuple-element.4, bf16[2560,8192]{1,0:T(8,128)(2,1)} %multiply_convert_fusion, s32[512]{0:T(512)S(1)} %iota_add_fusion.2, s32[1024]{0:T(1024)S(1)} %get-tuple-element.35), kind=kOutput, calls=%fused_computation.25 | convolution fusion | flops 8592031744 | bytes 29366272 | tf_op jit(solution)/shard_map/dot_general | solution.py:228
  310.0 1.2 slice_reduce_fusion
  (52 shorter events, 7.3 us)
Async XLA Ops:
  7.2 33.8 %all-gather.6.cloned.1.call-start = ((), (), s32[]{:S(2)}) async-start(), calls=%async_computation.1 | async-start | bytes 1341440 | tf_op jit(solution)/shard_map/all_gather | solution.py:173
  9.7 102.4 %all-gather.4.cloned.1.call-start = ((), (), s32[]{:S(2)}) async-start(), calls=%async_computation | async-start | bytes 9732096 | tf_op jit(solution)/shard_map/all_gather | solution.py:207
  9.8 6.8 %copy-start = (f32[2,1024,512]{2,1,0:T(8,128)S(1)}, f32[2,1024,512]{2,1,0:T(8,128)}, u32[]{:S(2)}) copy-start(f32[2,1024,512]{2,1,0:T(8,128)} %param.8) | copy-start | bytes 12582916
  44.0 0.8 copy-start.8
  44.8 1.9 copy-start.1
  44.8 1.9 copy-start.2
  44.8 1.9 copy-start.6
  44.9 1.9 copy-start.7
  46.8 6.3 %copy-start.5 = (f32[1,1,2,512]{3,1,2,0:T(1,128)S(1)}, f32[1,1,2,512]{3,1,2,0:T(1,128)}, u32[]{:S(2)}) copy-start(f32[1,1,2,512]{3,1,2,0:T(1,128)} %copy.14) | copy-start | bytes 12292
  293.6 17.6 %copy-start.3 = (f32[1024,128]{1,0:T(8,128)S(1)}, f32[1024,128]{1,0:T(8,128)}, u32[]{:S(2)}) copy-start(f32[1024,128]{1,0:T(8,128)} %get-tuple-element.5) | copy-start | bytes 1572868
  293.6 17.8 %copy-start.4 = (f32[1024]{0:T(1024)S(1)}, f32[1024]{0:T(1024)}, u32[]{:S(2)}) copy-start(f32[1024]{0:T(1024)} %param.11) | copy-start | bytes 12292
Sparse Core Ops, SparseCore 0:
  9.9 31.1 all-gather.5
  57.4 54.7 all-gather.3
